TPU v7x, 32 devices: a whole 2x2x4 slice. The times are simulated.
32 devices in a mesh: wide: 2 (over core), op: 16 (over z, y, x).
Axes of the slice: x: 2, y: 2, z: 4, core: 2. Of those that a mesh axis runs over, the one named last changes fastest.
Arguments:
- wavefunction: bfloat16 [32, 4, 512, 512], P('wide', None, 'op'), may hold values from -6 to 6
- left_ops: bfloat16 [128, 512, 512], P(('wide', 'op')), may hold values from -0.0390625 to 0.0390625
- right_ops: bfloat16 [128, 512, 512], P(('wide', 'op')), may hold values from -0.25 to 0.25
- in_sector: int32 [128], P(('wide', 'op')), may hold values from 0 to 31
- live_count: int32 [32], P(('wide', 'op')), may hold values from 2 to 4, as said below
Outputs:
- sigma_blocks: bfloat16 [2, 4, 512, 512], P('wide', None, 'op')
Inputs may be any that keep to these rules, and one draw needn't show every extreme that they name: `live_count`: in each aligned group of 16 entries (the devices of one op group), entries i and i + 8 sum to 6, and exactly 4 entries are 4.
All inputs are finite; a program needn't handle non-finite values.
Results may differ from a plain program's by a relative error of at most 0.0065.
Values may be sent and summed in bfloat16 or wider, within the bound.
A program may use at most 64 MiB of HBM per device.

v0:
```python
import jax
import jax.numpy as jnp
from jax import lax
from jax.sharding import PartitionSpec as P


def from_behind(x, axis, by):
    devices = lax.axis_size(axis)
    return lax.ppermute(x, axis, [(i, (i + by) % devices) for i in range(devices)])


def sandwich(sector, left_op, right_op):
    half_step = jnp.einsum(
        "smk,nk->smn", sector, right_op, preferred_element_type=jnp.float32
    ).astype(jnp.bfloat16)
    return jnp.einsum("im,smn->sin", left_op, half_step, preferred_element_type=jnp.float32)


def local(wavefunction, left_ops, right_ops, in_sector, live_count):
    group_size = lax.axis_size("op")
    slot_count = left_ops.shape[0]
    ins_all, live_all = (
        lax.all_gather(in_sector, "op", axis=0, tiled=True),
        lax.all_gather(live_count, "op", axis=0, tiled=True),
    )
    ins_grid = ins_all.reshape(group_size, slot_count)
    my_live = live_count[0]
    rows_all = lax.all_gather(wavefunction, "wide", axis=0, tiled=True)
    partner_ins = jnp.roll(ins_grid[:, slot_count - 1], group_size // 2)
    third_in = jnp.where(live_all >= 3, ins_grid[:, 2], partner_ins)
    work_grid = jnp.concatenate([ins_grid[:, :2], third_in[:, None]], axis=1)
    arrived_left, arrived_right = from_behind(
        (left_ops[slot_count - 1], right_ops[slot_count - 1]), "op", group_size // 2
    )
    own_third = my_live >= 3
    work_left = jnp.stack(
        [left_ops[0], left_ops[1], jnp.where(own_third, left_ops[2], arrived_left)]
    )
    work_right = jnp.stack(
        [right_ops[0], right_ops[1], jnp.where(own_third, right_ops[2], arrived_right)]
    )
    weights = [jnp.float32(1.0) for slot_index in range(slot_count - 1)]
    work_count = work_grid.shape[1]
    outgoing = jnp.take(rows_all, work_grid.reshape(-1), axis=0)
    arrived = lax.all_to_all(outgoing, "op", split_axis=0, concat_axis=2, tiled=True)
    partial_value = jnp.zeros(arrived.shape[1:], jnp.float32)
    for slot_index in range(work_count):
        partial_value = partial_value + weights[slot_index] * sandwich(
            arrived[slot_index], work_left[slot_index], work_right[slot_index]
        )
    summed = lax.psum_scatter(partial_value[None], "op", scatter_dimension=2, tiled=True)
    return summed.astype(jnp.bfloat16)


def solution(mesh):
    placed = (
        P("wide", None, "op", None),
        P(("wide", "op"), None, None),
        P(("wide", "op"), None, None),
        P(("wide", "op")),
        P(("wide", "op")),
    )
    return jax.shard_map(
        local, mesh=mesh, in_specs=placed, out_specs=P("wide", None, "op", None), check_vma=False
    )
```

profile of v0, /device:TPU:6, one launch (start us, length us, event | category | flops | bytes accessed | tf_op | source)
XLA Modules:
  0.0 429.7 jit_solution(4435426553336007252)
XLA Ops:
  6.5 0.0 copy-start.1
  6.5 0.0 copy-start.2
  6.5 0.0 all-gather.2.cloned.1.call-start
  6.5 0.7 all-gather.2.cloned.1.call-update
  7.9 0.0 copy-done.1
  7.9 0.6 fusion.34
  9.2 0.7 dynamic-update-slice.1
  9.9 0.0 copy-done.2
  9.9 0.2 dynamic-update-slice
  10.1 13.7 %all-reduce.3 = (s32[64]{0:T(128)S(1)}, s32[16]{0:T(128)S(1)}) all-reduce(s32[64]{0:T(128)S(1)} %dynamic-update-slice, s32[16]{0:T(128)S(1)} %dynamic-update-slice.1), channel_id=1, replica_groups=mesh['wide'=2,'op'=16] {'op'}, use_global_device_ids=true, to_apply=%add | all-reduce | flops 80 | bytes 640
  23.8 0.1 reshape.52
  23.9 0.2 slice_reduce_fusion.2
  24.1 0.2 slice_reduce_fusion
  24.3 0.1 fusion.31
  24.4 0.1 copy.29
  24.5 0.1 pad_add_fusion
  24.6 0.1 reshape.54
  24.7 0.1 reshape.53
  24.8 0.0 all-gather.2.cloned.1.call-done
  24.8 7.1 %gather_fusion = bf16[48,4,32,512]{3,2,1,0:T(8,128)(2,1)} fusion(bf16[32,4,32,512]{3,2,1,0:T(8,128)(2,1)} %all-gather.2.cloned.1.call-done, s32[1024]{0:T(1024)S(1)} %pad_clamp_fusion), kind=kCustom, calls=%fused_computation | custom fusion | bytes 12583104 | tf_op jit(solution)/shard_map/jit(_take)/gather | solution.py:44
  32.0 6.1 %broadcast_select_fusion = bf16[48,4,32,512]{3,2,1,0:T(8,128)(2,1)} fusion(bf16[48,4,32,512]{3,2,1,0:T(8,128)(2,1)} %gather_fusion, pred[48]{0:T(512)(128)(4,1)S(1)} %compare_and_fusion), kind=kLoop, calls=%fused_computation.1 | loop fusion | flops 3145728 | bytes 12582960 | tf_op jit(solution)/shard_map/jit(_take)/select_n | solution.py:44
  38.1 6.2 %all-to-all-start = ((bf16[48,4,32,512]{3,2,1,0:T(8,128)(2,1)}), bf16[48,4,32,512]{3,2,1,0:T(8,128)(2,1)}, u32[]{:S(2)}, u32[]{:S(2)}) async-start(bf16[48,4,32,512]{3,2,1,0:T(8,128)(2,1)} %broadcast_select_fusion), calls=%async_computation | async-start | bytes 12582912 | tf_op jit(solution)/shard_map/all_to_all | solution.py:45
  44.3 1.9 slice_bitcast_fusion.1
  46.2 2.4 collective-permute-start
  48.5 1.9 slice_bitcast_fusion
  50.4 0.6 collective-permute-start.1
  51.7 142.1 %all-to-all-done = bf16[48,4,32,512]{3,2,1,0:T(8,128)(2,1)} async-done(((bf16[48,4,32,512]{3,2,1,0:T(8,128)(2,1)}), bf16[48,4,32,512]{3,2,1,0:T(8,128)(2,1)}, u32[]{:S(2)}, u32[]{:S(2)}) %all-to-all-start) | async-done | bytes 6291488 | tf_op jit(solution)/shard_map/all_to_all | solution.py:45
  193.8 5.1 %fusion.33 = (bf16[1,4,16,32,512]{4,3,1,0,2:T(8,128)(2,1)}, bf16[1,4,16,32,512]{4,3,1,0,2:T(8,128)(2,1)S(1)}, bf16[1,4,16,32,512]{4,3,1,0,2:T(8,128)(2,1)S(1)}) fusion(bf16[3,4,16,32,512]{4,3,1,0,2:T(8,128)(2,1)} %bitcast.5), kind=kLoop, calls=%fused_computation.40 | loop fusion | bytes 12582912 | tf_op jit(solution)/shard_map/slice | solution.py:49
  198.9 1.6 copy.32
  200.5 6.1 %fusion.1 = f32[4,512,512]{2,1,0:T(8,128)} fusion(bf16[4,512,512]{2,1,0:T(8,128)(2,1)} %bitcast.64, bf16[4,512,512]{2,1,0:T(8,128)(2,1)} %param.6, bf16[4,512,512]{2,1,0:T(8,128)(2,1)} %param.7), kind=kOutput, calls=%fused_computation.4 | convolution fusion | flops 2148532224 | bytes 7340032 | tf_op jit(solution)/shard_map/im,smn->sin/dot_general | solution.py:16
  206.6 0.0 copy-start
  206.6 1.5 copy.30
  208.2 0.8 copy-done
  209.0 0.2 copy.34
  209.2 6.2 %fusion.3 = f32[4,512,512]{2,1,0:T(8,128)} fusion(bf16[4,512,512]{2,1,0:T(8,128)(2,1)} %bitcast.63, bf16[4,512,512]{2,1,0:T(8,128)(2,1)} %param.6, bf16[4,512,512]{2,1,0:T(8,128)(2,1)} %param.7), kind=kOutput, calls=%fused_computation.6 | convolution fusion | flops 2148532224 | bytes 7340032 | tf_op jit(solution)/shard_map/im,smn->sin/dot_general | solution.py:16
  215.4 5.3 %collective-permute-done = bf16[512,512]{1,0:T(8,128)(2,1)S(1)} collective-permute-done((bf16[512,512]{1,0:T(8,128)(2,1)}, bf16[512,512]{1,0:T(8,128)(2,1)S(1)}, u32[]{:S(2)}, u32[]{:S(2)}) %collective-permute-start) | collective-permute-done | bytes 524320 | tf_op jit(solution)/shard_map/ppermute | solution.py:9
  220.7 10.3 %collective-permute-done.1 = bf16[512,512]{1,0:T(8,128)(2,1)S(1)} collective-permute-done((bf16[512,512]{1,0:T(8,128)(2,1)}, bf16[512,512]{1,0:T(8,128)(2,1)S(1)}, u32[]{:S(2)}, u32[]{:S(2)}) %collective-permute-start.1) | collective-permute-done | bytes 524320 | tf_op jit(solution)/shard_map/ppermute | solution.py:9
  231.0 8.2 %add_bitcast_fusion = f32[1,4,512,512]{2,3,1,0:T(8,128)} fusion(f32[4,512,512]{2,1,0:T(8,128)} %fusion.3, f32[4,512,512]{2,1,0:T(8,128)} %fusion.1, bf16[4,512,512]{2,1,0:T(8,128)(2,1)S(1)} %bitcast.62, bf16[512,512]{1,0:T(8,128)(2,1)S(1)} %collective-permute-done.1, bf16[512,512]{1,0:T(8,128)(2,1)S(1)} %collective-permute-done, ...), kind=kOutput, calls=%fused_computation.2 | convolution fusion | flops 2151153664 | bytes 16778240 | tf_op jit(solution)/shard_map/im,smn->sin/dot_general | solution.py:16
  239.1 5.4 %copy.36 = f32[1,4,512,512]{3,1,0,2:T(4,128)} copy(f32[1,4,512,512]{2,3,1,0:T(8,128)} %add_bitcast_fusion) | data formatting | bytes 8388608 | tf_op jit(solution)/shard_map/broadcast_in_dim | solution.py:51
  244.6 177.5 %all-reduce.5 = bf16[1,4,512,512]{3,1,0,2:T(4,128)(2,1)S(1)} all-reduce(f32[1,4,512,512]{3,1,0,2:T(4,128)} %copy.36), channel_id=2, replica_groups=mesh['wide'=2,'op'=16] {'op'}, use_global_device_ids=true, to_apply=%region_0.1.clone | all-reduce | flops 1048576 | bytes 6291456
  422.1 0.1 dynamic-slice_convert_fusion
  422.2 0.7 copy.37
  (5 shorter events, 0.0 us)
Async XLA Ops:
  6.5 1.4 copy-start.1
  6.5 3.3 copy-start.2
  6.5 18.3 %all-gather.2.cloned.1.call-start = ((), (), s32[]{:S(2)}) async-start(), calls=%async_computation.1 | async-start | bytes 6291456 | tf_op jit(solution)/shard_map/all_gather | solution.py:28
  38.1 155.7 %all-to-all-start = ((bf16[48,4,32,512]{3,2,1,0:T(8,128)(2,1)}), bf16[48,4,32,512]{3,2,1,0:T(8,128)(2,1)}, u32[]{:S(2)}, u32[]{:S(2)}) async-start(bf16[48,4,32,512]{3,2,1,0:T(8,128)(2,1)} %broadcast_select_fusion), calls=%async_computation | async-start | bytes 12582912 | tf_op jit(solution)/shard_map/all_to_all | solution.py:45
  46.2 174.5 %collective-permute-start = (bf16[512,512]{1,0:T(8,128)(2,1)}, bf16[512,512]{1,0:T(8,128)(2,1)S(1)}, u32[]{:S(2)}, u32[]{:S(2)}) collective-permute-start(bf16[512,512]{1,0:T(8,128)(2,1)} %slice_bitcast_fusion.1), channel_id=1, source_target_pairs={{0,8},{1,9},{2,10},{3,11},{4,12},{5,13},{6,14},{7,15},{8,0},{9,1},... | collective-permute-start | bytes 1572872 | tf_op jit(solution)/shard_map/ppermute | solution.py:9
  50.4 180.5 %collective-permute-start.1 = (bf16[512,512]{1,0:T(8,128)(2,1)}, bf16[512,512]{1,0:T(8,128)(2,1)S(1)}, u32[]{:S(2)}, u32[]{:S(2)}) collective-permute-start(bf16[512,512]{1,0:T(8,128)(2,1)} %slice_bitcast_fusion), channel_id=1, source_target_pairs={{0,8},{1,9},{2,10},{3,11},{4,12},{5,13},{6,14},{7,15},{8,0},{9,1},... | collective-permute-start | bytes 1572872 | tf_op jit(solution)/shard_map/ppermute | solution.py:9
  206.6 2.3 copy-start
Sparse Core Ops, SparseCore 0:
  8.9 15.1 all-gather.1
where the time goes:
time: 433 us; the launch traced here: 430 us
  blocking collectives  191 us (44%)
  waiting for transfers between devices  158 us (36%)
  local copies, waits for them, and re-layouts  28.8 us (7%)
  matrix products  20.5 us (5%)
  between operations  15.4 us (4%)
  starting transfers between devices  9.1 us (2%)
  other arithmetic  6.28 us (1%)
    unnamed x2, blocking collectives  191 us
    all_to_all x1, waiting for transfers between devices, local(): lax.all_to_all(outgoing, 'op', split_axis=0, concat_axis=2, tiled=True)  142 us
    dot_general x3, matrix products, sandwich(): jnp.einsum('im,smn->sin', left_op, half_step, preferred_element_type=jnp....  20.5 us
    ppermute x2, waiting for transfers between devices, from_behind(): lax.ppermute(x, axis, [(i, (i + by) % devices) for i in range(devices)])  15.6 us
  transfers between devices with their start and end apart: 4, of which 3 were waited for; matrix products, arithmetic and copies ran while one was open for 6% of the time, Pallas kernels for 0%

commit v1 on v0

v1 whole, which is shorter than its diff:
```python
import jax
import jax.numpy as jnp
from jax import lax
from jax.sharding import PartitionSpec as P


def sandwich(sector, left_op, right_op):
    half_step = jnp.einsum(
        "smk,nk->smn", sector, right_op, preferred_element_type=jnp.float32
    ).astype(jnp.bfloat16)
    return jnp.einsum("im,smn->sin", left_op, half_step, preferred_element_type=jnp.float32)


def work_list(live, mine, theirs):
    third = jnp.where(live >= 3, mine[2], theirs[2])
    fourth = jnp.where(live >= 4, mine[3], jnp.where(live == 3, theirs[2], theirs[3]))
    return [mine[0], mine[1], theirs[0], theirs[1], third, fourth]


def local(wavefunction, left_ops, right_ops, in_sector, live_count):
    n = lax.axis_size("op")
    half_n = n // 2
    slots, size = left_ops.shape[0], left_ops.shape[1]
    me = lax.axis_index("op")
    side = me // half_n
    swap = [(i, (i + half_n) % n) for i in range(n)]
    split = size // 2
    left_mine = lax.dynamic_slice_in_dim(left_ops, side * split, split, axis=2)
    left_away = lax.dynamic_slice_in_dim(left_ops, (1 - side) * split, split, axis=2)
    right_theirs = lax.ppermute(right_ops, "op", swap)
    left_theirs = lax.ppermute(left_away, "op", swap)

    small = lax.all_gather(jnp.concatenate([in_sector, live_count]), "op", axis=0)
    ins, live = small[:, :slots], small[:, slots]
    rows = lax.all_gather(wavefunction, "wide", axis=0, tiled=True)
    partner = jnp.roll(ins, half_n, axis=0)
    grid = jnp.stack(work_list(live, ins.T, partner.T), axis=1)
    grid = lax.dynamic_slice_in_dim(grid, side * half_n, half_n, axis=0)
    outgoing = jnp.take(rows, grid.reshape(-1), axis=0)
    groups = [list(range(half_n)), list(range(half_n, n))]
    arrived = lax.all_to_all(
        outgoing, "op", split_axis=0, concat_axis=2, tiled=True, axis_index_groups=groups
    )
    lefts = work_list(live_count[0], left_mine, left_theirs)
    rights = work_list(live_count[0], right_ops, right_theirs)
    total = None
    for t in range(len(lefts)):
        term = sandwich(arrived[t], lefts[t], rights[t])
        total = term if total is None else total + term
    pieces = lax.all_to_all(
        total.astype(jnp.bfloat16).reshape(total.shape[0], n, size // n, size),
        "op", split_axis=1, concat_axis=1, tiled=True,
    )
    return jnp.sum(pieces.astype(jnp.float32), axis=1).astype(jnp.bfloat16)[None]


def solution(mesh):
    placed = (
        P("wide", None, "op", None),
        P(("wide", "op"), None, None),
        P(("wide", "op"), None, None),
        P(("wide", "op")),
        P(("wide", "op")),
    )
    return jax.shard_map(
        local, mesh=mesh, in_specs=placed, out_specs=P("wide", None, "op", None), check_vma=False
    )
```

time: 433 us -> 283 us (0.65)
  blocking collectives: 191 us -> 66.4 us
  waiting for transfers between devices: 158 us -> 133 us
  local copies, waits for them, and re-layouts: 28.8 us -> 16.8 us
  matrix products: 20.5 us -> 32 us
    unnamed x2 -> x1, blocking collectives: 191 us -> 13.7 us
    all_to_all x0 -> x1, blocking collectives: none -> 52.7 us  [local(): lax.all_to_all(total.astype(jnp.bfloat16).reshape(total.shape[0], n, size...]
    ppermute x2, waiting for transfers between devices: 15.6 us -> 0.01 us  [the longest x1 0.01 us: local(): left_theirs = lax.ppermute(left_away, 'op', swap)]
    dot_general x3 -> x6, matrix products: 20.5 us -> 32 us  [sandwich(): jnp.einsum('im,smn->sin', left_op, half_step, preferred_element_type=jnp....]
    all_to_all x1, waiting for transfers between devices: 142 us -> 132 us  [local(): lax.all_to_all(outgoing, 'op', split_axis=0, concat_axis=2, tiled=True, a...]
    broadcast_in_dim x2 -> x0, local copies, waits for them, and re-layouts: 5.53 us -> none  [the longest x1 5.44 us: local(): partial_value[None]]
    slice x6 -> x10, local copies, waits for them, and re-layouts: 8.9 us -> 6.95 us  [the longest x7 6.78 us: local(): term = sandwich(arrived[t], lefts[t], rights[t])]
  transfers between devices with their start and end apart: 4 -> 4, of which waited for: 3 -> 1; matrix products, arithmetic and copies ran while one was open for 6% -> 7% of each run, Pallas kernels for 0% -> 0%
where the time goes in v1:
time: 283 us; the launch traced here: 280 us
  waiting for transfers between devices  133 us (47%)
  blocking collectives  66.4 us (23%)
  matrix products  32 us (11%)
  local copies, waits for them, and re-layouts  16.8 us (6%)
  between operations  14.8 us (5%)
  starting transfers between devices  9.18 us (3%)
  other arithmetic  7.5 us (3%)
    all_to_all x1, waiting for transfers between devices, local(): lax.all_to_all(outgoing, 'op', split_axis=0, concat_axis=2, tiled=True, a...  132 us
    all_to_all x1, blocking collectives, local(): lax.all_to_all(total.astype(jnp.bfloat16).reshape(total.shape[0], n, size...  52.7 us
    dot_general x6, matrix products, sandwich(): jnp.einsum('im,smn->sin', left_op, half_step, preferred_element_type=jnp....  32 us
    unnamed x1, blocking collectives  13.7 us
    gather x1, local copies, waits for them, and re-layouts, local(): outgoing = jnp.take(rows, grid.reshape(-1), axis=0)  7.15 us
    slice x7, local copies, waits for them, and re-layouts, local(): term = sandwich(arrived[t], lefts[t], rights[t])  6.78 us
    all_to_all x1, starting transfers between devices, local(): lax.all_to_all(outgoing, 'op', split_axis=0, concat_axis=2, tiled=True, a...  6.26 us
    select_n x2, other arithmetic, local(): outgoing = jnp.take(rows, grid.reshape(-1), axis=0)  6.11 us
  transfers between devices with their start and end apart: 4, of which 1 were waited for; matrix products, arithmetic and copies ran while one was open for 7% of the time, Pallas kernels for 0%

profile of v1, /device:TPU:6, one launch (start us, length us, event | category | flops | bytes accessed | tf_op | source)
XLA Modules:
  0.0 279.6 jit_solution(1753668544848836886)
XLA Ops:
  6.5 0.0 all-gather.3.cloned.1.call-start
  6.5 0.7 all-gather.3.cloned.1.call-update
  7.9 0.0 copy-done.4
  7.9 0.6 dynamic-slice
  9.2 0.0 copy-done.3
  9.2 0.2 add_dynamic-update-slice_fusion
  9.4 13.7 %all-reduce = s32[80]{0:T(128)S(1)} all-reduce(s32[80]{0:T(128)S(1)} %add_dynamic-update-slice_fusion), channel_id=2, replica_groups=mesh['wide'=2,'op'=16] {'op'}, use_global_device_ids=true, to_apply=%add | all-reduce | flops 80 | bytes 640
  23.1 0.1 reshape.84
  23.2 0.1 copy.39
  23.3 0.1 copy.40
  23.3 0.1 add_bitcast_fusion
  23.4 0.1 copy.44
  23.5 0.1 copy.42
  23.6 0.1 copy.49
  23.7 0.1 copy.48
  23.8 0.1 slice_bitcast_fusion.12
  23.8 0.1 fusion.47
  23.9 0.1 stack.2
  24.0 0.1 reshape.74
  24.1 0.1 reshape.73
  24.2 0.0 all-gather.3.cloned.1.call-done
  24.2 7.1 %gather_fusion = bf16[48,4,32,512]{3,2,1,0:T(8,128)(2,1)} fusion(bf16[32,4,32,512]{3,2,1,0:T(8,128)(2,1)} %all-gather.3.cloned.1.call-done, s32[1024]{0:T(1024)S(1)} %pad_clamp_fusion), kind=kCustom, calls=%fused_computation | custom fusion | bytes 12583104 | tf_op jit(solution)/shard_map/jit(_take)/gather | solution.py:39
  31.4 6.1 %broadcast_select_fusion = bf16[48,4,32,512]{3,2,1,0:T(8,128)(2,1)} fusion(bf16[48,4,32,512]{3,2,1,0:T(8,128)(2,1)} %gather_fusion, pred[48]{0:T(512)(128)(4,1)S(1)} %compare_and_fusion), kind=kLoop, calls=%fused_computation.1 | loop fusion | flops 3145728 | bytes 12582960 | tf_op jit(solution)/shard_map/jit(_take)/select_n | solution.py:39
  37.5 6.3 %all-to-all-start = ((bf16[48,4,32,512]{3,2,1,0:T(8,128)(2,1)}), bf16[48,4,32,512]{3,2,1,0:T(8,128)(2,1)}, u32[]{:S(2)}, u32[]{:S(2)}) async-start(bf16[48,4,32,512]{3,2,1,0:T(8,128)(2,1)} %broadcast_select_fusion), calls=%async_computation | async-start | bytes 12582912 | tf_op jit(solution)/shard_map/all_to_all | solution.py:41
  43.8 1.2 collective-permute-start
  45.0 0.0 copy-done.2
  45.0 1.1 constant_dynamic-slice_fusion
  46.1 1.7 collective-permute-start.1
  47.8 132.1 %all-to-all-done = bf16[48,4,32,512]{3,2,1,0:T(8,128)(2,1)} async-done(((bf16[48,4,32,512]{3,2,1,0:T(8,128)(2,1)}), bf16[48,4,32,512]{3,2,1,0:T(8,128)(2,1)}, u32[]{:S(2)}, u32[]{:S(2)}) %all-to-all-start) | async-done | bytes 6291488 | tf_op jit(solution)/shard_map/all_to_all | solution.py:41
  179.9 3.4 %fusion.54 = (bf16[1,4,8,32,512]{4,3,1,0,2:T(8,128)(2,1)S(1)}, bf16[1,4,8,32,512]{4,3,1,0,2:T(8,128)(2,1)S(1)}, bf16[1,4,8,32,512]{4,3,1,0,2:T(8,128)(2,1)S(1)},...) fusion(bf16[6,4,8,32,512]{4,3,1,0,2:T(8,128)(2,1)} %bitcast.13), kind=kLoop, calls=%fused_computation.72 | loop fusion | bytes 12582912 | tf_op jit(solution)/shard_map/slice | solution.py:48
  183.3 1.1 copy.55
  184.4 0.1 copy.54
  184.4 0.1 copy.53
  184.5 1.0 copy.52
  185.6 0.1 copy.51
  185.6 1.0 copy.50
  186.7 4.7 %fusion = f32[4,512,512]{1,2,0:T(8,128)} fusion(bf16[4,256,512]{2,1,0:T(8,128)(2,1)} %bitcast.108, bf16[4,512,512]{2,1,0:T(8,128)(2,1)} %param.7, bf16[4,512,512]{2,1,0:T(8,128)(2,1)} %param.6, s32[]{:T(128)S(6)} %select_n.109), kind=kOutput, calls=%fused_computation.9 | convolution fusion | flops 1074266112 | bytes 6029316 | tf_op jit(solution)/shard_map/im,smn->sin/dot_general | solution.py:11
  191.3 4.4 %fusion.1 = f32[4,512,512]{1,2,0:T(8,128)} fusion(bf16[4,256,512]{2,1,0:T(8,128)(2,1)S(1)} %bitcast.105, bf16[4,512,512]{2,1,0:T(8,128)(2,1)} %param.7, bf16[4,512,512]{2,1,0:T(8,128)(2,1)} %param.6, s32[]{:T(128)S(6)} %add.70, s32[]{:T(128)S(6)} %select_n.109), kind=kOutput, calls=%fused_computation.10 | convolution fusion | flops 1074266112 | bytes 6029320 | tf_op jit(solution)/shard_map/im,smn->sin/dot_general | solution.py:11
  195.7 0.0 collective-permute-done.1
  195.7 0.0 collective-permute-done
  195.7 4.5 %fusion.3 = f32[4,512,512]{1,2,0:T(8,128)} fusion(bf16[4,256,512]{2,1,0:T(8,128)(2,1)S(1)} %bitcast.106, bf16[4,512,512]{2,1,0:T(8,128)(2,1)} %collective-permute-done, bf16[4,512,256]{2,1,0:T(8,128)(2,1)} %collective-permute-done.1), kind=kOutput, calls=%fused_computation.12 | convolution fusion | flops 1074266112 | bytes 6029312 | tf_op jit(solution)/shard_map/im,smn->sin/dot_general | solution.py:11
  200.2 0.0 copy-done
  200.2 4.4 %fusion.2 = f32[4,512,512]{1,2,0:T(8,128)} fusion(bf16[4,256,512]{2,1,0:T(8,128)(2,1)S(1)} %bitcast.107, bf16[4,512,512]{2,1,0:T(8,128)(2,1)} %collective-permute-done, bf16[4,512,256]{2,1,0:T(8,128)(2,1)} %collective-permute-done.1), kind=kOutput, calls=%fused_computation.11 | convolution fusion | flops 1074266112 | bytes 6029312 | tf_op jit(solution)/shard_map/im,smn->sin/dot_general | solution.py:11
  204.5 4.7 %fusion.4 = f32[4,512,512]{1,2,0:T(8,128)} fusion(bf16[4,256,512]{2,1,0:T(8,128)(2,1)S(1)} %bitcast.104, bf16[4,512,512]{2,1,0:T(8,128)(2,1)} %param.7, pred[]{:T(512)} %bitcast.36, bf16[4,512,512]{2,1,0:T(8,128)(2,1)} %collective-permute-done, bf16[4,512,512]{2,1,0:T(8,128)(2,1)} %param.6, s32[]{:T(128)S(6)} %add.71, s32[]{:T(128)S(6)} %select_n.109, ...), kind=kOutput, calls=%fused_computation.13 | convolution fusion | flops 1074659328 | bytes 6816776 | tf_op jit(solution)/shard_map/im,smn->sin/dot_general | solution.py:11
  209.2 9.5 %add_convert_fusion = bf16[4,512,512]{1,2,0:T(8,128)(2,1)S(1)} fusion(f32[4,512,512]{1,2,0:T(8,128)} %fusion.4, f32[4,512,512]{1,2,0:T(8,128)} %fusion.3, f32[4,512,512]{1,2,0:T(8,128)} %fusion.2, f32[4,512,512]{1,2,0:T(8,128)} %fusion, f32[4,512,512]{1,2,0:T(8,128)} %fusion.1, bf16[4,256,512]{2,1,0:T(8,128)(2,1)S(1)} %bitcast.109, ...), kind=kOutput, calls=%fused_computation.2 | convolution fusion | flops 1081344000 | bytes 26478600 | tf_op jit(solution)/shard_map/im,smn->sin/dot_general | solution.py:11
  218.7 0.2 copy.56
  219.0 52.7 %all_to_all.20 = bf16[4,16,32,512]{3,2,0,1:T(8,128)(2,1)S(1)} all-to-all(bf16[4,16,32,512]{3,2,0,1:T(8,128)(2,1)S(1)} %copy.56), channel_id=1, replica_groups=mesh['wide'=2,'op'=16] {'op'}, dimensions={1} | all-to-all | bytes 4194304 | tf_op jit(solution)/shard_map/all_to_all | solution.py:50
  271.7 1.1 reduce_sum.12
  (14 shorter events, 0.1 us)
Async XLA Ops:
  6.5 1.4 copy-start.4
  6.5 2.6 copy-start.3
  6.5 17.7 %all-gather.3.cloned.1.call-start = ((), (), s32[]{:S(2)}) async-start(), calls=%async_computation.2 | async-start | bytes 6291456 | tf_op jit(solution)/shard_map/all_gather | solution.py:35
  37.5 7.5 %copy-start.2 = (bf16[4,512,512]{2,1,0:T(8,128)(2,1)S(1)}, bf16[4,512,512]{2,1,0:T(8,128)(2,1)}, u32[]{:S(2)}) copy-start(bf16[4,512,512]{2,1,0:T(8,128)(2,1)} %param.6) | copy-start | bytes 6291460
  37.5 142.4 %all-to-all-start = ((bf16[48,4,32,512]{3,2,1,0:T(8,128)(2,1)}), bf16[48,4,32,512]{3,2,1,0:T(8,128)(2,1)}, u32[]{:S(2)}, u32[]{:S(2)}) async-start(bf16[48,4,32,512]{3,2,1,0:T(8,128)(2,1)} %broadcast_select_fusion), calls=%async_computation | async-start | bytes 12582912 | tf_op jit(solution)/shard_map/all_to_all | solution.py:41
  43.8 152.0 %collective-permute-start = (bf16[4,512,512]{2,1,0:T(8,128)(2,1)}, bf16[4,512,512]{2,1,0:T(8,128)(2,1)}, u32[]{:S(2)}, u32[]{:S(2)}) collective-permute-start(bf16[4,512,512]{2,1,0:T(8,128)(2,1)} %param.7), channel_id=1, source_target_pairs={{0,8},{1,9},{2,10},{3,11},{4,12},{5,13},{6,14},{7,15},{8,0},{9,1},... | collective-permute-start | bytes 6291464 | tf_op jit(solution)/shard_map/ppermute | solution.py:30
  46.1 149.6 %collective-permute-start.1 = (bf16[4,512,256]{2,1,0:T(8,128)(2,1)}, bf16[4,512,256]{2,1,0:T(8,128)(2,1)}, u32[]{:S(2)}, u32[]{:S(2)}) collective-permute-start(bf16[4,512,256]{2,1,0:T(8,128)(2,1)} %constant_dynamic-slice_fusion), channel_id=1, source_target_pairs={{0,8},{1,9},{2,10},{3,11},{4,12},{5,13},{6,14},{7,15},{8,0},{9,1},... | collective-permute-start | bytes 3145736 | tf_op jit(solution)/shard_map/ppermute | solution.py:31
  195.7 4.5 %copy-start = (bf16[1,4,8,32,512]{4,3,2,1,0:T(8,128)(2,1)S(1)}, bf16[1,4,8,32,512]{4,3,2,1,0:T(8,128)(2,1)}, u32[]{:S(2)}) copy-start(bf16[1,4,8,32,512]{4,3,2,1,0:T(8,128)(2,1)} %copy.52) | copy-start | bytes 3145732
  204.5 4.7 %copy-start.1 = (bf16[1,4,8,32,512]{4,3,2,1,0:T(8,128)(2,1)S(1)}, bf16[1,4,8,32,512]{4,3,2,1,0:T(8,128)(2,1)}, u32[]{:S(2)}) copy-start(bf16[1,4,8,32,512]{4,3,2,1,0:T(8,128)(2,1)} %copy.55) | copy-start | bytes 3145732
Sparse Core Ops, SparseCore 0:
  8.9 15.1 all-gather.2

commit v2 on v1

v2 whole, which is shorter than its diff:
```python
import functools

import jax
import jax.numpy as jnp
from jax import lax
from jax.experimental import pallas as pl
from jax.experimental.pallas import tpu as pltpu
from jax.sharding import PartitionSpec as P

MESH = pl.DeviceIdType.MESH
WORK = 6


def work_list(live, mine, theirs):
    third = jnp.where(live >= 3, mine[2], theirs[2])
    fourth = jnp.where(live >= 4, mine[3], jnp.where(live == 3, theirs[2], theirs[3]))
    return [mine[0], mine[1], theirs[0], theirs[1], third, fourth]


def kernel(
    n, wides, table, wf, lefts, rights, out,
    rows, outgoing, arrived, left_v, right_v, acc, red_out, red_in, swap_out, swap_in,
    local_sem, wide_sem, op_send, op_recv, a2a_send, a2a_recv, red_send, red_recv, swap_sem,
):
    h = n // 2
    w = lax.axis_index("wide")
    me = lax.axis_index("op")
    side = lax.div(me, h)
    r = lax.rem(me, h)
    base = side * h
    partner = lax.rem(me + h, n)
    sectors, states, depth, size = wf.shape
    slots = lefts.shape[0]
    split = size // 2

    barrier = pltpu.get_barrier_semaphore()

    def greet(k, c):
        to = base + lax.rem(r + k, h)
        pl.semaphore_signal(barrier, inc=1, device_id=(w, to), device_id_type=MESH)
        return c

    other = 1 - w
    pl.semaphore_signal(barrier, inc=1, device_id=(w, partner), device_id_type=MESH)
    pl.semaphore_signal(barrier, inc=1, device_id=(other, me), device_id_type=MESH)
    lax.fori_loop(1, h, greet, 0)

    my_cols = pl.ds(pl.multiple_of(side * split, split), split)
    away_cols = pl.ds(pl.multiple_of((1 - side) * split, split), split)
    my_sectors = pl.ds(w * sectors, sectors)
    own_rows = pltpu.make_async_copy(wf, rows.at[my_sectors], local_sem.at[0])
    own_right = pltpu.make_async_copy(rights, right_v.at[pl.ds(0, slots)], local_sem.at[1])
    own_left = pltpu.make_async_copy(
        lefts.at[:, :, my_cols], left_v.at[pl.ds(0, slots)], local_sem.at[2]
    )
    own_rows.start()
    own_right.start()
    own_left.start()
    pl.semaphore_wait(barrier, h + 1)

    def remote(src, dst, ssem, rsem, to):
        return pltpu.make_async_remote_copy(
            src_ref=src, dst_ref=dst, send_sem=ssem, recv_sem=rsem,
            device_id=to, device_id_type=MESH,
        )

    wide_copy = remote(wf, rows.at[my_sectors], wide_sem.at[0], wide_sem.at[1], (other, me))
    wide_copy.start()
    right_copies = [
        remote(rights.at[j], right_v.at[slots + j], op_send.at[0, j], op_recv.at[0, j], (w, partner))
        for j in range(slots)
    ]
    left_copies = [
        remote(
            lefts.at[j, :, away_cols], left_v.at[slots + j],
            op_send.at[1, j], op_recv.at[1, j], (w, partner),
        )
        for j in range(slots)
    ]
    right_copies[0].start()
    left_copies[0].start()
    own_rows.wait()
    wide_copy.wait()

    def fill(t):
        def one(e, c):
            outgoing[t, e] = rows[table[e * WORK + t]]
            return c

        lax.fori_loop(0, h, one, 0)
        arrived[t, r] = rows[table[h * WORK + 2 + t]]

    def a2a(t, k):
        e = lax.rem(r + k, h)
        return remote(
            outgoing.at[t, e], arrived.at[t, r], a2a_send.at[t, e], a2a_recv.at[t, r], (w, base + e)
        )

    def a2a_from(t, k):
        e = lax.rem(r + k, h)
        return remote(
            outgoing.at[t, e], arrived.at[t, e], a2a_send.at[t, e], a2a_recv.at[t, e], (w, base + e)
        )

    def each(action):
        def step(k, c):
            action(k)
            return c

        lax.fori_loop(1, h, step, 0)

    for t in range(WORK):
        fill(t)
        if t:
            each(lambda k: a2a(t - 1, k).start())
    each(lambda k: a2a(WORK - 1, k).start())
    for j in range(1, slots):
        right_copies[j].start()
        left_copies[j].start()

    def compute(t, at, first=False):
        def one(s, c):
            x = arrived[t, :, s]
            if depth % 16:
                x = x.astype(jnp.float32)
            x = x.reshape(h * depth, size).astype(jnp.bfloat16)
            half = lax.dot_general(
                x, right_v[at], (((1,), (1,)), ((), ())), preferred_element_type=jnp.float32
            ).astype(jnp.bfloat16)
            term = jnp.dot(left_v[at], half, preferred_element_type=jnp.float32)
            acc[s] = term if first else acc[s] + term
            return c

        lax.fori_loop(0, states, one, 0)

    own_right.wait()
    own_left.wait()
    for t in range(2):
        each(lambda k: a2a_from(t, k).wait_recv())
        compute(t, t, first=t == 0)
    for t in range(2, 4):
        each(lambda k: a2a_from(t, k).wait_recv())
        right_copies[t - 2].wait_recv()
        left_copies[t - 2].wait_recv()
        compute(t, slots + t - 2)
    for t in range(4, WORK):
        each(lambda k: a2a_from(t, k).wait_recv())
    for j in range(2, slots):
        right_copies[j].wait_recv()
        left_copies[j].wait_recv()
    for t in range(4, WORK):
        compute(t, table[h * WORK + t - 4])

    def pack(e, c):
        for p in range(2):
            at = pl.ds(pl.multiple_of((p * h + e) * depth, depth), depth)
            red_out[e, p] = acc[:, at, :].astype(jnp.bfloat16)
        return c

    def red(k):
        e = lax.rem(r + k, h)
        return remote(red_out.at[e], red_in.at[r], red_send.at[e], red_recv.at[r], (w, base + e))

    def red_from(k):
        e = lax.rem(r + k, h)
        return remote(red_out.at[e], red_in.at[e], red_send.at[e], red_recv.at[e], (w, base + e))

    lax.fori_loop(0, h, pack, 0)
    each(lambda k: red(k).start())
    each(lambda k: red_from(k).wait_recv())

    def mine(p):
        at = pl.ds(pl.multiple_of((p * h + r) * depth, depth), depth)
        start = acc[:, at, :]

        def add(k, total):
            return total + red_in[lax.rem(r + k, h), p].astype(jnp.float32)

        return lax.fori_loop(1, h, add, start)

    swap_out[...] = mine(1 - side).astype(jnp.bfloat16)
    swap = remote(swap_out, swap_in, swap_sem.at[0], swap_sem.at[1], (w, partner))
    swap.start()
    kept = mine(side)
    swap.wait()
    out[...] = (kept + swap_in[...].astype(jnp.float32)).astype(jnp.bfloat16)
    for t in range(WORK):
        each(lambda k: a2a(t, k).wait_send())
    each(lambda k: red(k).wait_send())
    for j in range(slots):
        right_copies[j].wait_send()
        left_copies[j].wait_send()


def local(wavefunction, left_ops, right_ops, in_sector, live_count):
    n, wides = lax.axis_size("op"), lax.axis_size("wide")
    h = n // 2
    slots, size = left_ops.shape[0], left_ops.shape[1]
    sectors, states, depth, _ = wavefunction.shape
    me = lax.axis_index("op")
    side, r = me // h, me % h
    small = lax.all_gather(jnp.concatenate([in_sector, live_count]), "op", axis=0)
    ins, live = small[:, :slots], small[:, slots]
    grid = jnp.stack(work_list(live, ins.T, jnp.roll(ins, h, axis=0).T), axis=1)
    grid = lax.dynamic_slice_in_dim(grid, side * h, h, axis=0)
    my_live = live_count[0]
    third = jnp.where(my_live >= 3, 2, slots + 2)
    fourth = jnp.where(my_live >= 4, 3, jnp.where(my_live == 3, slots + 2, slots + 3))
    own = lax.dynamic_index_in_dim(grid, r, 0, keepdims=False)
    table = jnp.concatenate([grid.reshape(-1), jnp.stack([third, fourth]), own]).astype(jnp.int32)
    dma = pltpu.SemaphoreType.DMA
    half_size = size // 2
    out = pl.pallas_call(
        functools.partial(kernel, n, wides),
        out_shape=jax.ShapeDtypeStruct((states, depth, size), jnp.bfloat16),
        in_specs=[pl.BlockSpec(memory_space=pltpu.SMEM)]
        + [pl.BlockSpec(memory_space=pl.ANY)] * 3,
        out_specs=pl.BlockSpec(memory_space=pltpu.VMEM),
        scratch_shapes=[
            pltpu.VMEM((wides * sectors, states, depth, size), jnp.bfloat16),
            pltpu.VMEM((WORK, h, states, depth, size), jnp.bfloat16),
            pltpu.VMEM((WORK, h, states, depth, size), jnp.bfloat16),
            pltpu.VMEM((2 * slots, size, half_size), jnp.bfloat16),
            pltpu.VMEM((2 * slots, size, size), jnp.bfloat16),
            pltpu.VMEM((states, size, size), jnp.float32),
            pltpu.VMEM((h, 2, states, depth, size), jnp.bfloat16),
            pltpu.VMEM((h, 2, states, depth, size), jnp.bfloat16),
            pltpu.VMEM((states, depth, size), jnp.bfloat16),
            pltpu.VMEM((states, depth, size), jnp.bfloat16),
            dma((3,)), dma((2,)), dma((2, slots)), dma((2, slots)),
            dma((WORK, h)), dma((WORK, h)), dma((h,)), dma((h,)), dma((2,)),
        ],
        compiler_params=pltpu.CompilerParams(
            collective_id=0, has_side_effects=True, vmem_limit_bytes=60 * 1024 * 1024
        ),
    )(table, wavefunction, left_ops, right_ops)
    return out[None]


def solution(mesh):
    placed = (
        P("wide", None, "op", None),
        P(("wide", "op"), None, None),
        P(("wide", "op"), None, None),
        P(("wide", "op")),
        P(("wide", "op")),
    )
    return jax.shard_map(
        local, mesh=mesh, in_specs=placed, out_specs=P("wide", None, "op", None), check_vma=False
    )
```

time: 283 us -> 211 us (0.75); the launches traced: 280 us -> 211 us
  Pallas kernels: 0 us -> 191 us
  waiting for transfers between devices: 133 us -> 0 us
  blocking collectives: 66.4 us -> 13.7 us
  matrix products: 32 us -> 0 us
  between operations: 14.8 us -> 1.37 us
  local copies, waits for them, and re-layouts: 16.8 us -> 3.67 us
  starting transfers between devices: 9.18 us -> 0 us
  other arithmetic: 7.5 us -> 1.57 us
    pallas_call x0 -> x1, Pallas kernels: none -> 191 us  [local(): pl.pallas_call(functools.partial(kernel, n, wides), out_shape=jax.ShapeDt...]
    all_to_all x1 -> x0, waiting for transfers between devices: 132 us -> none  [local(): lax.all_to_all(outgoing, 'op', split_axis=0, concat_axis=2, tiled=True, a...]
    all_to_all x1 -> x0, blocking collectives: 52.7 us -> none  [local(): lax.all_to_all(total.astype(jnp.bfloat16).reshape(total.shape[0], n, size...]
    dot_general x6 -> x0, matrix products: 32 us -> none  [sandwich(): jnp.einsum('im,smn->sin', left_op, half_step, preferred_element_type=jnp....]
    gather x1 -> x0, local copies, waits for them, and re-layouts: 7.15 us -> none  [local(): outgoing = jnp.take(rows, grid.reshape(-1), axis=0)]
    slice x10 -> x3, local copies, waits for them, and re-layouts: 6.95 us -> 0.17 us  [local(): grid = jnp.stack(work_list(live, ins.T, jnp.roll(ins, h, axis=0).T), axis=1)]
    all_to_all x1 -> x0, starting transfers between devices: 6.26 us -> none  [local(): lax.all_to_all(outgoing, 'op', split_axis=0, concat_axis=2, tiled=True, a...]
    select_n x2 -> x0, other arithmetic: 6.11 us -> none  [local(): outgoing = jnp.take(rows, grid.reshape(-1), axis=0)]
  transfers between devices with their start and end apart: 4 -> 0, of which waited for: 1 -> 0; matrix products, arithmetic and copies ran while one was open for 7% -> 0% of each run, Pallas kernels for 0% -> 0%
where the time goes in v2:
time: 211 us
  Pallas kernels  191 us (91%)
  blocking collectives  13.7 us (6%)
  local copies, waits for them, and re-layouts  3.67 us (2%)
    pallas_call x1, Pallas kernels, local(): pl.pallas_call(functools.partial(kernel, n, wides), out_shape=jax.ShapeDt...  191 us
    unnamed x1, blocking collectives  13.7 us

profile of v2, /device:TPU:6, one launch (start us, length us, event | category | flops | bytes accessed | tf_op | source)
XLA Modules:
  0.0 211.2 jit_solution(15762721142754720376)
XLA Ops:
  0.7 1.2 dynamic-slice
  2.6 0.8 add_dynamic-update-slice_fusion
  3.4 13.7 %all-reduce = s32[80]{0:T(128)S(1)} all-reduce(s32[80]{0:T(128)S(1)} %add_dynamic-update-slice_fusion), channel_id=2, replica_groups=mesh['wide'=2,'op'=16] {'op'}, use_global_device_ids=true, to_apply=%add | all-reduce | flops 80 | bytes 640
  17.1 0.1 reshape.25
  17.2 0.1 copy.24
  17.3 0.1 copy.25
  17.4 0.1 add_bitcast_fusion
  17.5 0.1 copy.29
  17.5 0.1 copy.27
  17.6 0.1 fusion
  17.7 0.1 copy.34
  17.8 0.1 copy.33
  17.9 0.1 slice_bitcast_fusion.2
  17.9 0.1 stack.2
  18.1 0.1 reshape.24
  18.2 0.6 pad_add_fusion.table
  18.7 190.8 %shard_map.55 = bf16[4,32,512]{2,1,0:T(8,128)(2,1)} custom-call(s32[56]{0:T(128)} %pad_add_fusion.table, bf16[16,4,32,512]{3,2,1,0:T(8,128)(2,1)} %wf.1, bf16[4,512,512]{2,1,0:T(8,128)(2,1)} %lefts.1, bf16[4,512,512]{2,1,0:T(8,128)(2,1)} %rights.1), custom_call_target="tpu_custom_call" | custom-call | tf_op jit(solution)/shard_map/pallas_call | solution.py:213
  209.6 1.6 copy.38
  (6 shorter events, 0.0 us)

commit v3 on v1

v3 whole, which is shorter than its diff:
```python
import functools

import jax
import jax.numpy as jnp
from jax import lax
from jax.experimental import pallas as pl
from jax.experimental.pallas import tpu as pltpu
from jax.sharding import PartitionSpec as P

MESH = pl.DeviceIdType.MESH
WORK = 6
BLOCKS = 4


def kernel(
    n, small, wf, lefts, rights, out,
    info, table, rows, outgoing, arrived, left_v, right_0, right_1, right_2, right_3,
    acc, red_out, red_in, swap_out, swap_in,
    local_sem, wide_sem, info_send, info_recv, left_send, left_recv, right_send, right_recv,
    a2a_send, a2a_recv, red_send, red_recv, swap_send, swap_recv,
):
    h = n // 2
    w = lax.axis_index("wide")
    me = lax.axis_index("op")
    side = lax.div(me, h)
    r = lax.rem(me, h)
    base = side * h
    partner = lax.rem(me + h, n)
    sectors, states, depth, size = wf.shape
    slots = lefts.shape[0]
    split = size // 2
    width = size // BLOCKS
    right_v = (right_0, right_1, right_2, right_3)

    def each(count, action):
        def step(k, c):
            action(k)
            return c

        lax.fori_loop(1, count, step, 0)

    barrier = pltpu.get_barrier_semaphore()
    other = 1 - w
    pl.semaphore_signal(barrier, inc=1, device_id=(other, me), device_id_type=MESH)
    each(n, lambda k: pl.semaphore_signal(
        barrier, inc=1, device_id=(w, lax.rem(me + k, n)), device_id_type=MESH))

    my_cols = pl.ds(pl.multiple_of(side * split, split), split)
    away_cols = pl.ds(pl.multiple_of((1 - side) * split, split), split)
    my_sectors = pl.ds(w * sectors, sectors)
    local_copies = [
        pltpu.make_async_copy(wf, rows.at[my_sectors], local_sem.at[0]),
        pltpu.make_async_copy(
            lefts.at[:, :, my_cols], left_v.at[pl.ds(0, slots)], local_sem.at[1]
        ),
    ] + [
        pltpu.make_async_copy(
            rights.at[:, pl.ds(q * width, width), :],
            right_v[q].at[pl.ds(0, slots)], local_sem.at[2 + q],
        )
        for q in range(BLOCKS)
    ]
    for copy in local_copies:
        copy.start()
    info[me] = small[...]
    pl.semaphore_wait(barrier, n)

    def remote(src, dst, ssem, rsem, to):
        return pltpu.make_async_remote_copy(
            src_ref=src, dst_ref=dst, send_sem=ssem, recv_sem=rsem,
            device_id=to, device_id_type=MESH,
        )

    def tell(k, at):
        to = lax.rem(me + k, n)
        row = me if at is None else to
        return remote(small, info.at[row], info_send.at[to], info_recv.at[row], (w, to))

    each(n, lambda k: tell(k, None).start())
    wide_copy = remote(wf, rows.at[my_sectors], wide_sem.at[0], wide_sem.at[1], (other, me))
    wide_copy.start()
    left_copies = [
        remote(
            lefts.at[j, :, away_cols], left_v.at[slots + j],
            left_send.at[j], left_recv.at[j], (w, partner),
        )
        for j in range(slots)
    ]
    right_copies = [
        [
            remote(
                rights.at[j, pl.ds(q * width, width), :], right_v[q].at[slots + j],
                right_send.at[q, j], right_recv.at[q, j], (w, partner),
            )
            for j in range(slots)
        ]
        for q in range(BLOCKS)
    ]
    inner = lax.rem(lax.div(4 * me, n) + 1, 4) >= 2

    def start_ops(blocks):
        for q in blocks:
            for copy in right_copies[q]:
                copy.start()

    for copy in left_copies:
        copy.start()

    @pl.when(inner)
    def _():
        start_ops(range(BLOCKS))
    each(n, lambda k: tell(k, 1).wait_recv())
    to_scalars = pltpu.make_async_copy(info, table, local_sem.at[2 + BLOCKS])
    to_scalars.start()
    to_scalars.wait()
    local_copies[0].wait()
    wide_copy.wait()

    def sector(t, e):
        d = base + e
        p = lax.rem(d + h, n)
        live = table[d, 0, slots]
        if t < 2:
            return table[d, 0, t]
        if t < 4:
            return table[p, 0, t - 2]
        if t == 4:
            return jnp.where(live >= 3, table[d, 0, 2], table[p, 0, 2])
        third = jnp.where(live == 3, table[p, 0, 2], table[p, 0, 3])
        return jnp.where(live >= 4, table[d, 0, 3], third)

    def fill(t):
        def one(e, c):
            outgoing[t, e] = rows[sector(t, e)]
            return c

        lax.fori_loop(0, h, one, 0)
        arrived[t, r] = rows[sector(t, r)]

    def a2a(t, k, incoming=False):
        e = lax.rem(r + k, h)
        at = e if incoming else r
        return remote(
            outgoing.at[t, e], arrived.at[t, at], a2a_send.at[t, e], a2a_recv.at[t, at], (w, base + e)
        )

    for t in range(WORK):
        fill(t)
        if t:
            each(h, lambda k: a2a(t - 1, k).start())
    each(h, lambda k: a2a(WORK - 1, k).start())

    @pl.when(jnp.logical_not(inner))
    def _():
        start_ops(range(BLOCKS))

    def compute(t, at, q, first=False):
        x = arrived[t]
        if depth % 16:
            x = x.astype(jnp.float32)
        x = x.reshape(h * states * depth, size).astype(jnp.bfloat16)
        half = lax.dot_general(
            x, right_v[q][at], (((1,), (1,)), ((), ())), preferred_element_type=jnp.float32
        ).reshape(h, states, depth, width)
        left = left_v[at]
        for s in range(states):
            mid = half[:, s].reshape(h * depth, width).astype(jnp.bfloat16)
            term = jnp.dot(left, mid, preferred_element_type=jnp.float32)
            acc[q, s] = term if first else acc[q, s] + term

    for copy in local_copies[1:]:
        copy.wait()
    for t in range(2):
        each(h, lambda k: a2a(t, k, True).wait_recv())
        for q in range(BLOCKS):
            compute(t, t, q, first=t == 0)
    for t in range(2, WORK):
        each(h, lambda k: a2a(t, k, True).wait_recv())
    for copy in left_copies:
        copy.wait_recv()

    my_live = table[me, 0, slots]
    third = jnp.where(my_live >= 3, 2, slots + 2)
    fourth = jnp.where(my_live >= 4, 3, jnp.where(my_live == 3, slots + 2, slots + 3))

    def red(q, k, incoming=False):
        e = lax.rem(r + k, h)
        at = e if incoming else r
        return remote(
            red_out.at[q, e], red_in.at[q, at], red_send.at[q, e], red_recv.at[q, at], (w, base + e)
        )

    def swap(q):
        return remote(swap_out.at[q], swap_in.at[q], swap_send.at[q], swap_recv.at[q], (w, partner))

    def mine(q, p):
        at = pl.ds(pl.multiple_of((p * h + r) * depth, depth), depth)

        def add(k, total):
            return total + red_in[q, lax.rem(r + k, h), p].astype(jnp.float32)

        return lax.fori_loop(1, h, add, acc[q, :, at, :])

    def finish(q):
        each(h, lambda k: red(q, k, True).wait_recv())
        swap_out[q] = mine(q, 1 - side).astype(jnp.bfloat16)
        swap(q).start()

    for q in range(BLOCKS):
        for copy in right_copies[q]:
            copy.wait_recv()
        compute(2, slots, q)
        compute(3, slots + 1, q)
        compute(4, third, q)
        compute(5, fourth, q)

        def pack(e, c):
            for p in range(2):
                at = pl.ds(pl.multiple_of((p * h + e) * depth, depth), depth)
                red_out[q, e, p] = acc[q, :, at, :].astype(jnp.bfloat16)
            return c

        lax.fori_loop(0, h, pack, 0)
        each(h, lambda k: red(q, k).start())
        if q:
            finish(q - 1)
    finish(BLOCKS - 1)
    for q in range(BLOCKS):
        kept = mine(q, side)
        swap(q).wait()
        out[:, :, pl.ds(q * width, width)] = (kept + swap_in[q].astype(jnp.float32)).astype(jnp.bfloat16)
    for t in range(WORK):
        each(h, lambda k: a2a(t, k).wait_send())
    for q in range(BLOCKS):
        each(h, lambda k: red(q, k).wait_send())
        for copy in right_copies[q]:
            copy.wait_send()
    for copy in left_copies:
        copy.wait_send()
    each(n, lambda k: tell(k, None).wait_send())


def local(wavefunction, left_ops, right_ops, in_sector, live_count):
    n, wides = lax.axis_size("op"), lax.axis_size("wide")
    h = n // 2
    slots, size = left_ops.shape[0], left_ops.shape[1]
    sectors, states, depth, _ = wavefunction.shape
    width = size // BLOCKS
    small = jnp.concatenate([in_sector, live_count])
    small = jnp.pad(small, (0, 128 - small.shape[0]))[None]
    dma = pltpu.SemaphoreType.DMA
    bf16, f32 = jnp.bfloat16, jnp.float32
    out = pl.pallas_call(
        functools.partial(kernel, n),
        out_shape=jax.ShapeDtypeStruct((states, depth, size), bf16),
        in_specs=[pl.BlockSpec(memory_space=pltpu.VMEM)]
        + [pl.BlockSpec(memory_space=pl.ANY)] * 3,
        out_specs=pl.BlockSpec(memory_space=pltpu.VMEM),
        scratch_shapes=[
            pltpu.VMEM((n, 1, 128), jnp.int32),
            pltpu.SMEM((n, 1, 128), jnp.int32),
            pltpu.VMEM((wides * sectors, states, depth, size), bf16),
            pltpu.VMEM((WORK, h, states, depth, size), bf16),
            pltpu.VMEM((WORK, h, states, depth, size), bf16),
            pltpu.VMEM((2 * slots, size, size // 2), bf16),
        ]
        + [pltpu.VMEM((2 * slots, width, size), bf16) for q in range(BLOCKS)]
        + [
            pltpu.VMEM((BLOCKS, states, size, width), f32),
            pltpu.VMEM((BLOCKS, h, 2, states, depth, width), bf16),
            pltpu.VMEM((BLOCKS, h, 2, states, depth, width), bf16),
            pltpu.VMEM((BLOCKS, states, depth, width), bf16),
            pltpu.VMEM((BLOCKS, states, depth, width), bf16),
            dma((3 + BLOCKS,)), dma((2,)), dma((n,)), dma((n,)), dma((slots,)), dma((slots,)),
            dma((BLOCKS, slots)), dma((BLOCKS, slots)), dma((WORK, h)), dma((WORK, h)),
            dma((BLOCKS, h)), dma((BLOCKS, h)), dma((BLOCKS,)), dma((BLOCKS,)),
        ],
        compiler_params=pltpu.CompilerParams(
            collective_id=0, has_side_effects=True, vmem_limit_bytes=60 * 1024 * 1024
        ),
    )(small, wavefunction, left_ops, right_ops)
    return out[None]


def solution(mesh):
    placed = (
        P("wide", None, "op", None),
        P(("wide", "op"), None, None),
        P(("wide", "op"), None, None),
        P(("wide", "op")),
        P(("wide", "op")),
    )
    return jax.shard_map(
        local, mesh=mesh, in_specs=placed, out_specs=P("wide", None, "op", None), check_vma=False
    )
```

time: 283 us -> 195 us (0.69)
  Pallas kernels: 0 us -> 191 us
  waiting for transfers between devices: 133 us -> 0 us
  blocking collectives: 66.4 us -> 0 us
  matrix products: 32 us -> 0 us
  local copies, waits for them, and re-layouts: 16.8 us -> 2.08 us
  between operations: 14.8 us -> 0.66 us
  starting transfers between devices: 9.18 us -> 0 us
  other arithmetic: 7.5 us -> 0.73 us
    pallas_call x0 -> x1, Pallas kernels: none -> 191 us  [local(): pl.pallas_call(functools.partial(kernel, n), out_shape=jax.ShapeDtypeStru...]
    all_to_all x1 -> x0, waiting for transfers between devices: 132 us -> none  [local(): lax.all_to_all(outgoing, 'op', split_axis=0, concat_axis=2, tiled=True, a...]
    all_to_all x1 -> x0, blocking collectives: 52.7 us -> none  [local(): lax.all_to_all(total.astype(jnp.bfloat16).reshape(total.shape[0], n, size...]
    dot_general x6 -> x0, matrix products: 32 us -> none  [sandwich(): jnp.einsum('im,smn->sin', left_op, half_step, preferred_element_type=jnp....]
    unnamed x1 -> x0, blocking collectives: 13.7 us -> none
    gather x1 -> x0, local copies, waits for them, and re-layouts: 7.15 us -> none  [local(): outgoing = jnp.take(rows, grid.reshape(-1), axis=0)]
    slice x10 -> x0, local copies, waits for them, and re-layouts: 6.95 us -> none  [the longest x7 6.78 us: local(): term = sandwich(arrived[t], lefts[t], rights[t])]
    all_to_all x1 -> x0, starting transfers between devices: 6.26 us -> none  [local(): lax.all_to_all(outgoing, 'op', split_axis=0, concat_axis=2, tiled=True, a...]
  transfers between devices with their start and end apart: 4 -> 0, of which waited for: 1 -> 0; matrix products, arithmetic and copies ran while one was open for 7% -> 0% of each run, Pallas kernels for 0% -> 0%
where the time goes in v3:
time: 195 us; the launch traced here: 194 us
  Pallas kernels  191 us (98%)
  local copies, waits for them, and re-layouts  2.08 us (1%)
    pallas_call x1, Pallas kernels, local(): pl.pallas_call(functools.partial(kernel, n), out_shape=jax.ShapeDtypeStru...  191 us

profile of v3, /device:TPU:6, one launch (start us, length us, event | category | flops | bytes accessed | tf_op | source)
XLA Modules:
  0.0 194.2 jit_solution(11325058349738035494)
XLA Ops:
  0.7 0.7 pad_add_fusion
  1.4 0.5 pad_bitcast_fusion.small
  1.9 190.7 %shard_map.55 = bf16[4,32,512]{2,1,0:T(8,128)(2,1)} custom-call(s32[1,128]{1,0:T(1,128)} %pad_bitcast_fusion.small, bf16[16,4,32,512]{3,2,1,0:T(8,128)(2,1)} %wf.1, bf16[4,512,512]{2,1,0:T(8,128)(2,1)} %lefts.1, bf16[4,512,512]{2,1,0:T(8,128)(2,1)} %rights.1), custom_call_target="tpu_custom_call" | custom-call | tf_op jit(solution)/shard_map/pallas_call | solution.py:253
  192.6 1.6 copy.8

commit v4 on v3

--- a/solution.py
+++ b/solution.py
@@ -15,9 +15,9 @@
 def kernel(
     n, small, wf, lefts, rights, out,
     info, table, rows, outgoing, arrived, left_v, right_0, right_1, right_2, right_3,
-    acc, red_out, red_in, swap_out, swap_in,
+    acc, red_out, red_in, mid_out, mid_in, swap_out, swap_in,
     local_sem, wide_sem, info_send, info_recv, left_send, left_recv, right_send, right_recv,
-    a2a_send, a2a_recv, red_send, red_recv, swap_send, swap_recv,
+    a2a_send, a2a_recv, red_send, red_recv, mid_send, mid_recv, swap_send, swap_recv,
 ):
     h = n // 2
     w = lax.axis_index("wide")
@@ -30,6 +30,11 @@
     slots = lefts.shape[0]
     split = size // 2
     width = size // BLOCKS
+    plane = n // 4
+    z = lax.div(me, plane)
+    rp = lax.rem(me, plane)
+    zl = lax.rem(z, 2)
+    neighbour = base + lax.rem(r + plane, h)
     right_v = (right_0, right_1, right_2, right_3)
 
     def each(count, action):
@@ -184,26 +189,39 @@
     fourth = jnp.where(my_live >= 4, 3, jnp.where(my_live == 3, slots + 2, slots + 3))
 
     def red(q, k, incoming=False):
-        e = lax.rem(r + k, h)
-        at = e if incoming else r
+        e = lax.rem(rp + k, plane)
+        at = e if incoming else rp
         return remote(
-            red_out.at[q, e], red_in.at[q, at], red_send.at[q, e], red_recv.at[q, at], (w, base + e)
-        )
+            red_out.at[q, e], red_in.at[q, at], red_send.at[q, e], red_recv.at[q, at],
+            (w, z * plane + e),
+        )
+
+    def step(q):
+        return remote(mid_out.at[q], mid_in.at[q], mid_send.at[q], mid_recv.at[q], (w, neighbour))
 
     def swap(q):
         return remote(swap_out.at[q], swap_in.at[q], swap_send.at[q], swap_recv.at[q], (w, partner))
 
-    def mine(q, p):
-        at = pl.ds(pl.multiple_of((p * h + r) * depth, depth), depth)
+    def mine(q, zo):
+        at = pl.ds(pl.multiple_of((zo * plane + rp) * depth, depth), depth)
 
         def add(k, total):
-            return total + red_in[q, lax.rem(r + k, h), p].astype(jnp.float32)
-
-        return lax.fori_loop(1, h, add, acc[q, :, at, :])
-
-    def finish(q):
-        each(h, lambda k: red(q, k, True).wait_recv())
-        swap_out[q] = mine(q, 1 - side).astype(jnp.bfloat16)
+            return total + red_in[q, lax.rem(rp + k, plane), zo].astype(jnp.float32)
+
+        return lax.fori_loop(1, plane, add, acc[q, :, at, :])
+
+    def second(q):
+        each(plane, lambda k: red(q, k, True).wait_recv())
+        for p in range(2):
+            mid_out[q, p] = mine(q, 2 * p + 1 - zl).astype(jnp.bfloat16)
+        step(q).start()
+
+    def both(q, p):
+        return mine(q, 2 * p + zl) + mid_in[q, p].astype(jnp.float32)
+
+    def third_step(q):
+        step(q).wait_recv()
+        swap_out[q] = both(q, 1 - side).astype(jnp.bfloat16)
         swap(q).start()
 
     for q in range(BLOCKS):
@@ -215,24 +233,29 @@
         compute(5, fourth, q)
 
         def pack(e, c):
-            for p in range(2):
-                at = pl.ds(pl.multiple_of((p * h + e) * depth, depth), depth)
-                red_out[q, e, p] = acc[q, :, at, :].astype(jnp.bfloat16)
+            for zo in range(4):
+                at = pl.ds(pl.multiple_of((zo * plane + e) * depth, depth), depth)
+                red_out[q, e, zo] = acc[q, :, at, :].astype(jnp.bfloat16)
             return c
 
-        lax.fori_loop(0, h, pack, 0)
-        each(h, lambda k: red(q, k).start())
+        lax.fori_loop(0, plane, pack, 0)
+        each(plane, lambda k: red(q, k).start())
         if q:
-            finish(q - 1)
-    finish(BLOCKS - 1)
+            second(q - 1)
+        if q > 1:
+            third_step(q - 2)
+    second(BLOCKS - 1)
+    for q in range(max(0, BLOCKS - 2), BLOCKS):
+        third_step(q)
     for q in range(BLOCKS):
-        kept = mine(q, side)
+        kept = both(q, side)
         swap(q).wait()
         out[:, :, pl.ds(q * width, width)] = (kept + swap_in[q].astype(jnp.float32)).astype(jnp.bfloat16)
     for t in range(WORK):
         each(h, lambda k: a2a(t, k).wait_send())
     for q in range(BLOCKS):
-        each(h, lambda k: red(q, k).wait_send())
+        each(plane, lambda k: red(q, k).wait_send())
+        step(q).wait_send()
         for copy in right_copies[q]:
             copy.wait_send()
     for copy in left_copies:
@@ -267,13 +290,16 @@
         + [pltpu.VMEM((2 * slots, width, size), bf16) for q in range(BLOCKS)]
         + [
             pltpu.VMEM((BLOCKS, states, size, width), f32),
-            pltpu.VMEM((BLOCKS, h, 2, states, depth, width), bf16),
-            pltpu.VMEM((BLOCKS, h, 2, states, depth, width), bf16),
+            pltpu.VMEM((BLOCKS, n // 4, 4, states, depth, width), bf16),
+            pltpu.VMEM((BLOCKS, n // 4, 4, states, depth, width), bf16),
+            pltpu.VMEM((BLOCKS, 2, states, depth, width), bf16),
+            pltpu.VMEM((BLOCKS, 2, states, depth, width), bf16),
             pltpu.VMEM((BLOCKS, states, depth, width), bf16),
             pltpu.VMEM((BLOCKS, states, depth, width), bf16),
             dma((3 + BLOCKS,)), dma((2,)), dma((n,)), dma((n,)), dma((slots,)), dma((slots,)),
             dma((BLOCKS, slots)), dma((BLOCKS, slots)), dma((WORK, h)), dma((WORK, h)),
-            dma((BLOCKS, h)), dma((BLOCKS, h)), dma((BLOCKS,)), dma((BLOCKS,)),
+            dma((BLOCKS, n // 4)), dma((BLOCKS, n // 4)),
+            dma((BLOCKS,)), dma((BLOCKS,)), dma((BLOCKS,)), dma((BLOCKS,)),
         ],
         compiler_params=pltpu.CompilerParams(
             collective_id=0, has_side_effects=True, vmem_limit_bytes=60 * 1024 * 1024

time: 195 us -> 190 us (0.974)
  Pallas kernels: 191 us -> 184 us
    pallas_call x1, Pallas kernels: 191 us -> 184 us  [local(): pl.pallas_call(functools.partial(kernel, n), out_shape=jax.ShapeDtypeStru...]
where the time goes in v4:
time: 190 us; the launch traced here: 187 us
  Pallas kernels  184 us (97%)
  local copies, waits for them, and re-layouts  2.08 us (1%)
    pallas_call x1, Pallas kernels, local(): pl.pallas_call(functools.partial(kernel, n), out_shape=jax.ShapeDtypeStru...  184 us

profile of v4, /device:TPU:6, one launch (start us, length us, event | category | flops | bytes accessed | tf_op | source)
XLA Modules:
  0.0 187.3 jit_solution(1929389850897533027)
XLA Ops:
  0.7 0.7 pad_add_fusion
  1.4 0.5 pad_bitcast_fusion.small
  1.9 183.8 %shard_map.55 = bf16[4,32,512]{2,1,0:T(8,128)(2,1)} custom-call(s32[1,128]{1,0:T(1,128)} %pad_bitcast_fusion.small, bf16[16,4,32,512]{3,2,1,0:T(8,128)(2,1)} %wf.1, bf16[4,512,512]{2,1,0:T(8,128)(2,1)} %lefts.1, bf16[4,512,512]{2,1,0:T(8,128)(2,1)} %rights.1), custom_call_target="tpu_custom_call" | custom-call | tf_op jit(solution)/shard_map/pallas_call | solution.py:276
  185.7 1.6 copy.8

commit v5 on v4

--- a/solution.py
+++ b/solution.py
@@ -14,7 +14,7 @@
 
 def kernel(
     n, small, wf, lefts, rights, out,
-    info, table, rows, outgoing, arrived, left_v, right_0, right_1, right_2, right_3,
+    info, table, rows, far, outgoing, arrived, left_v, right_0, right_1, right_2, right_3,
     acc, red_out, red_in, mid_out, mid_in, swap_out, swap_in,
     local_sem, wide_sem, info_send, info_recv, left_send, left_recv, right_send, right_recv,
     a2a_send, a2a_recv, red_send, red_recv, mid_send, mid_recv, swap_send, swap_recv,
@@ -83,7 +83,12 @@
 
     each(n, lambda k: tell(k, None).start())
     wide_copy = remote(wf, rows.at[my_sectors], wide_sem.at[0], wide_sem.at[1], (other, me))
+    slab = remote(wf, far.at[my_sectors], wide_sem.at[2], wide_sem.at[3], (w, neighbour))
+    slab.start()
     wide_copy.start()
+    relay = remote(
+        far.at[my_sectors], far.at[my_sectors], wide_sem.at[4], wide_sem.at[5], (other, me)
+    )
     left_copies = [
         remote(
             lefts.at[j, :, away_cols], left_v.at[slots + j],
@@ -101,19 +106,12 @@
         ]
         for q in range(BLOCKS)
     ]
-    inner = lax.rem(lax.div(4 * me, n) + 1, 4) >= 2
-
-    def start_ops(blocks):
-        for q in blocks:
-            for copy in right_copies[q]:
-                copy.start()
-
     for copy in left_copies:
         copy.start()
-
-    @pl.when(inner)
-    def _():
-        start_ops(range(BLOCKS))
+    for block in right_copies:
+        for copy in block:
+            copy.start()
+
     each(n, lambda k: tell(k, 1).wait_recv())
     to_scalars = pltpu.make_async_copy(info, table, local_sem.at[2 + BLOCKS])
     to_scalars.start()
@@ -134,30 +132,41 @@
         third = jnp.where(live == 3, table[p, 0, 2], table[p, 0, 3])
         return jnp.where(live >= 4, table[d, 0, 3], third)
 
-    def fill(t):
+    def fill(t, near):
+        held, at = (rows, zl) if near else (far, 1 - zl)
+
         def one(e, c):
-            outgoing[t, e] = rows[sector(t, e)]
+            outgoing[t, at * plane + e] = held[sector(t, zl * plane + e)]
             return c
 
-        lax.fori_loop(0, h, one, 0)
-        arrived[t, r] = rows[sector(t, r)]
-
-    def a2a(t, k, incoming=False):
-        e = lax.rem(r + k, h)
-        at = e if incoming else r
+        lax.fori_loop(0, plane, one, 0)
+        arrived[t, at * plane + rp] = held[sector(t, r)]
+
+    def a2a(t, near, k, incoming=False):
+        e = lax.rem(rp + k, plane)
+        held = (zl if near else 1 - zl) * plane
+        at = held + (e if incoming else rp)
         return remote(
-            outgoing.at[t, e], arrived.at[t, at], a2a_send.at[t, e], a2a_recv.at[t, at], (w, base + e)
-        )
-
-    for t in range(WORK):
-        fill(t)
-        if t:
-            each(h, lambda k: a2a(t - 1, k).start())
-    each(h, lambda k: a2a(WORK - 1, k).start())
-
-    @pl.when(jnp.logical_not(inner))
-    def _():
-        start_ops(range(BLOCKS))
+            outgoing.at[t, held + e], arrived.at[t, at], a2a_send.at[t, held + e], a2a_recv.at[t, at],
+            (w, z * plane + e),
+        )
+
+    def arrive(t):
+        for near in (True, False):
+            each(plane, lambda k: a2a(t, near, k, True).wait_recv())
+
+    def send_all(near):
+        for t in range(WORK):
+            fill(t, near)
+            if t:
+                each(plane, lambda k: a2a(t - 1, near, k).start())
+        each(plane, lambda k: a2a(WORK - 1, near, k).start())
+
+    send_all(True)
+    slab.wait_recv()
+    relay.start()
+    relay.wait()
+    send_all(False)
 
     def compute(t, at, q, first=False):
         x = arrived[t]
@@ -176,11 +185,11 @@
     for copy in local_copies[1:]:
         copy.wait()
     for t in range(2):
-        each(h, lambda k: a2a(t, k, True).wait_recv())
+        arrive(t)
         for q in range(BLOCKS):
             compute(t, t, q, first=t == 0)
     for t in range(2, WORK):
-        each(h, lambda k: a2a(t, k, True).wait_recv())
+        arrive(t)
     for copy in left_copies:
         copy.wait_recv()
 
@@ -252,7 +261,8 @@
         swap(q).wait()
         out[:, :, pl.ds(q * width, width)] = (kept + swap_in[q].astype(jnp.float32)).astype(jnp.bfloat16)
     for t in range(WORK):
-        each(h, lambda k: a2a(t, k).wait_send())
+        for near in (True, False):
+            each(plane, lambda k: a2a(t, near, k).wait_send())
     for q in range(BLOCKS):
         each(plane, lambda k: red(q, k).wait_send())
         step(q).wait_send()
@@ -261,6 +271,7 @@
     for copy in left_copies:
         copy.wait_send()
     each(n, lambda k: tell(k, None).wait_send())
+    slab.wait_send()
 
 
 def local(wavefunction, left_ops, right_ops, in_sector, live_count):
@@ -283,6 +294,7 @@
             pltpu.VMEM((n, 1, 128), jnp.int32),
             pltpu.SMEM((n, 1, 128), jnp.int32),
             pltpu.VMEM((wides * sectors, states, depth, size), bf16),
+            pltpu.VMEM((wides * sectors, states, depth, size), bf16),
             pltpu.VMEM((WORK, h, states, depth, size), bf16),
             pltpu.VMEM((WORK, h, states, depth, size), bf16),
             pltpu.VMEM((2 * slots, size, size // 2), bf16),
@@ -296,7 +308,7 @@
             pltpu.VMEM((BLOCKS, 2, states, depth, width), bf16),
             pltpu.VMEM((BLOCKS, states, depth, width), bf16),
             pltpu.VMEM((BLOCKS, states, depth, width), bf16),
-            dma((3 + BLOCKS,)), dma((2,)), dma((n,)), dma((n,)), dma((slots,)), dma((slots,)),
+            dma((3 + BLOCKS,)), dma((6,)), dma((n,)), dma((n,)), dma((slots,)), dma((slots,)),
             dma((BLOCKS, slots)), dma((BLOCKS, slots)), dma((WORK, h)), dma((WORK, h)),
             dma((BLOCKS, n // 4)), dma((BLOCKS, n // 4)),
             dma((BLOCKS,)), dma((BLOCKS,)), dma((BLOCKS,)), dma((BLOCKS,)),

time: 190 us -> 181 us (0.953)
  Pallas kernels: 184 us -> 174 us
    pallas_call x1, Pallas kernels: 184 us -> 174 us  [local(): pl.pallas_call(functools.partial(kernel, n), out_shape=jax.ShapeDtypeStru...]
where the time goes in v5:
time: 181 us; the launch traced here: 178 us
  Pallas kernels  174 us (96%)
  local copies, waits for them, and re-layouts  2.08 us (1%)
    pallas_call x1, Pallas kernels, local(): pl.pallas_call(functools.partial(kernel, n), out_shape=jax.ShapeDtypeStru...  174 us

profile of v5, /device:TPU:6, one launch (start us, length us, event | category | flops | bytes accessed | tf_op | source)
XLA Modules:
  0.0 178.0 jit_solution(7602046023608058892)
XLA Ops:
  0.7 0.7 pad_add_fusion
  1.4 0.5 pad_bitcast_fusion.small
  1.9 174.5 %shard_map.55 = bf16[4,32,512]{2,1,0:T(8,128)(2,1)} custom-call(s32[1,128]{1,0:T(1,128)} %pad_bitcast_fusion.small, bf16[16,4,32,512]{3,2,1,0:T(8,128)(2,1)} %wf.1, bf16[4,512,512]{2,1,0:T(8,128)(2,1)} %lefts.1, bf16[4,512,512]{2,1,0:T(8,128)(2,1)} %rights.1), custom_call_target="tpu_custom_call" | custom-call | tf_op jit(solution)/shard_map/pallas_call | solution.py:287
  176.4 1.6 copy.8
